TPU v7x, 32 devices: a whole 2x2x4 slice. The times are simulated.
32 devices in a mesh: dp: 4 (over z), feat: 8 (over y, x, core).
Axes of the slice: x: 2, y: 2, z: 4, core: 2. Of those that a mesh axis runs over, the one named last changes fastest.
Arguments:
- clip_feats: bfloat16 [2, 384, 8192], P(None, 'dp', 'feat'), may hold values from 0 to 60
- proj_weight: bfloat16 [8192, 8192], P('dp', 'feat'), may hold values from -0.0625 to 0.0625
Outputs:
- loss_value: float32 [], replicated
- weight_grad: float32 [8192, 8192], P('dp', 'feat')
- redundancy: float32 [], replicated
- pair_similarity: float32 [384, 384], P('dp')
All inputs are finite; a program needn't handle non-finite values.
Results may differ from a plain program's by a relative error of at most 0.034.
Values may be sent and summed in bfloat16 or wider, within the bound.
A program may use at most 64 MiB of HBM per device.

v0:
```python
import math
import jax
import jax.numpy as jnp
from jax import lax
from jax.sharding import PartitionSpec as P

D = 8192
off_weight = 0.0051
epsilon = 1e-05
grad_scale = 32.0


def per_device(clip_feats, proj_weight):
    pairs = clip_feats.shape[1]
    width = clip_feats.shape[2]
    dp_count = lax.axis_size("dp")
    pair_count = float(pairs * dp_count)
    gathered = lax.all_gather(clip_feats, "feat", axis=2, tiled=True)
    stacked = gathered.reshape(2 * pairs, gathered.shape[2])
    projected = jnp.dot(
        stacked,
        lax.all_gather(proj_weight, "dp", axis=0, tiled=True),
        preferred_element_type=jnp.float32,
    ).reshape(2, pairs, width)
    col_mean = lax.psum(jnp.sum(projected, axis=1), "dp")[:, None, :] / pair_count
    centered = projected - col_mean
    col_var = lax.psum(jnp.sum(centered * centered, axis=1), "dp")[:, None, :] / pair_count
    col_scale = lax.rsqrt(col_var + epsilon)
    normed = centered * col_scale
    quantized = normed.astype(jnp.bfloat16)
    widened = quantized.astype(jnp.float32)
    batch_all = lax.all_gather(quantized, "dp", axis=1, tiled=True)
    gram_part = jnp.einsum("vpc,vnc->vpn", quantized, batch_all, preferred_element_type=jnp.float32)
    grams = lax.psum(gram_part, "feat")
    total_pairs = grams.shape[2]
    row_ids = (
        lax.broadcasted_iota(jnp.int32, (pairs, total_pairs), 0) + lax.axis_index("dp") * pairs
    )
    col_ids = lax.broadcasted_iota(jnp.int32, (pairs, total_pairs), 1)
    pair_similarity = jnp.where(
        row_ids == col_ids, 0.0, (grams[0] + grams[1]) / (2.0 * math.sqrt(float(D)))
    )
    diag_corr = lax.psum(jnp.sum(widened[0] * widened[1], axis=0), "dp") / pair_count
    frobenius = jnp.sum(grams[0] * grams[1])
    diag_term = jnp.sum((1.0 - diag_corr) ** 2 - off_weight * diag_corr * diag_corr)
    dp_first = (lax.axis_index("dp") == 0).astype(jnp.float32)
    feat_first = (lax.axis_index("feat") == 0).astype(jnp.float32)
    frob_scaled = feat_first * frobenius / (pair_count * pair_count)
    loss_term = dp_first * diag_term + off_weight * frob_scaled
    off_term = frob_scaled - dp_first * jnp.sum(diag_corr * diag_corr)
    total_loss, off_sum = lax.psum((loss_term, off_term), ("dp", "feat"))
    loss_value = 16.0 * total_loss / float(D)
    redundancy = 8.0 * pair_count * off_sum / (float(D) * float(D))
    slope = -2.0 * (1.0 - diag_corr) - 2.0 * off_weight * diag_corr
    coefficient = 2.0 * off_weight / (pair_count * pair_count)
    gram_q = grams.astype(jnp.bfloat16)
    cross_first = jnp.dot(gram_q[1], batch_all[0], preferred_element_type=jnp.float32)
    cross_second = jnp.dot(gram_q[0], batch_all[1], preferred_element_type=jnp.float32)
    grad_norm = jnp.stack(
        [
            slope * widened[1] / pair_count + coefficient * cross_first,
            slope * widened[0] / pair_count + coefficient * cross_second,
        ]
    )
    sum_one, sum_two = lax.psum(
        (jnp.sum(grad_norm, axis=1), jnp.sum(grad_norm * normed, axis=1)), "dp"
    )
    pre_grad = col_scale * (
        grad_norm - sum_one[:, None, :] / pair_count - normed * (sum_two[:, None, :] / pair_count)
    )
    pre_q = pre_grad.astype(jnp.bfloat16)
    flat_grad = pre_q.reshape(2 * pairs, width)
    summed = lax.psum_scatter(
        jnp.dot(stacked.T, flat_grad, preferred_element_type=jnp.float32).astype(jnp.bfloat16),
        "dp",
        scatter_dimension=0,
        tiled=True,
    ).astype(jnp.float32)
    return (loss_value, grad_scale * summed, redundancy, pair_similarity)


def solution(mesh):
    placed = (P(None, "dp", "feat"), P("dp", "feat"))
    return jax.shard_map(
        per_device,
        mesh=mesh,
        in_specs=placed,
        out_specs=(P(), P("dp", "feat"), P(), P("dp", None)),
        check_vma=False,
    )
```

profile of v0, /device:TPU:0, one launch (start us, length us, event | category | flops | bytes accessed | tf_op | source)
XLA Modules:
  0.0 791.4 jit_solution(3627898898711487195)
XLA Ops:
  7.2 0.7 all-gather.4.cloned.1.call-update
  7.9 0.7 all-gather.6.cloned.1.call-update
  8.7 36.3 %all-gather.4.cloned.1.call-done = bf16[2,96,8192]{2,1,0:T(8,128)(2,1)} async-done(((bf16[2,96,1024]{2,1,0:T(8,128)(2,1)}), bf16[2,96,8192]{2,1,0:T(8,128)(2,1)}) %all-gather.4.cloned.1.call-update) | async-done | bytes 3145744 | tf_op jit(solution)/shard_map/all_gather | solution.py:18
  45.0 288.4 %all-gather.6.cloned.1.call-done = bf16[8192,1024]{1,0:T(8,128)(2,1)} async-done(((bf16[2048,1024]{1,0:T(8,128)(2,1)}), bf16[8192,1024]{1,0:T(8,128)(2,1)}) %all-gather.6.cloned.1.call-update) | async-done | bytes 16777232 | tf_op jit(solution)/shard_map/all_gather | solution.py:22
  333.3 8.5 %fusion.16 = (f32[2,1024]{1,0:T(2,128)S(1)}, f32[2,96,1024]{2,1,0:T(8,128)S(1)}) fusion(bf16[2,96,8192]{2,1,0:T(8,128)(2,1)} %all-gather.4.cloned.1.call-done, bf16[8192,1024]{1,0:T(8,128)(2,1)} %all-gather.6.cloned.1.call-done), kind=kOutput, calls=%fused_computation.42 | convolution fusion | flops 3221420032 | bytes 20717568 | tf_op jit(solution)/shard_map/dot_general | solution.py:20
  341.8 8.8 %psum.56 = f32[2,1024]{1,0:T(2,128)S(1)} all-reduce(f32[2,1024]{1,0:T(2,128)S(1)} %get-tuple-element.19), channel_id=1, replica_groups=mesh['dp'=4,'feat'=8] {'dp'}, use_global_device_ids=true, to_apply=%region_1.0 | all-reduce | flops 2048 | bytes 16384 | tf_op jit(solution)/shard_map/psum | solution.py:25
  350.7 10.3 %psum.57 = f32[2,1024]{1,0:T(2,128)S(1)} all-reduce(f32[2,1024]{1,0:T(2,128)S(1)} %multiply_reduce_fusion.1), channel_id=1, replica_groups=mesh['dp'=4,'feat'=8] {'dp'}, use_global_device_ids=true, to_apply=%region_3.0 | all-reduce | flops 2048 | bytes 16384 | tf_op jit(solution)/shard_map/psum | solution.py:27
  361.1 0.9 fusion.14
  362.1 8.7 %psum.58 = f32[1024]{0:T(1024)S(1)} all-reduce(f32[1024]{0:T(1024)S(1)} %multiply_reduce_fusion.2), channel_id=1, replica_groups=mesh['dp'=4,'feat'=8] {'dp'}, use_global_device_ids=true, to_apply=%region_5.6 | all-reduce | flops 1024 | bytes 8192 | tf_op jit(solution)/shard_map/psum | solution.py:43
  370.8 26.6 %all-gather.8.cloned.1.call-done = bf16[2,384,1024]{2,1,0:T(8,128)(2,1)} async-done(((bf16[2,96,1024]{2,1,0:T(8,128)(2,1)}), bf16[2,384,1024]{2,1,0:T(8,128)(2,1)}) %all-gather.8.cloned.1.call-update) | async-done | bytes 1572880 | tf_op jit(solution)/shard_map/all_gather | solution.py:32
  397.3 3.0 fusion.17
  400.4 1.2 multiply_reduce_fusion.4
  401.6 50.8 %all-reduce.4.cloned.1.call-done = f32[2,96,384]{2,1,0:T(8,128)} async-done(((f32[2,96,384]{2,1,0:T(8,128)}), f32[2,96,384]{2,1,0:T(8,128)}) %all-reduce.4.cloned.1.call-update) | async-done | bytes 294928 | tf_op jit(solution)/shard_map/psum | solution.py:34
  452.4 1.0 convert_element_type.25
  453.4 1.4 fusion.4
  454.8 1.0 fusion.6
  455.8 0.7 copy-done.1
  456.8 18.7 %all-reduce.1 = (f32[2,1024]{1,0:T(2,128)S(1)}, f32[2,1024]{1,0:T(2,128)S(1)}) all-reduce(f32[2,1024]{1,0:T(2,128)S(1)} %get-tuple-element.9, f32[2,1024]{1,0:T(2,128)S(1)} %get-tuple-element.8), channel_id=1, replica_groups=mesh['dp'=4,'feat'=8] {'dp'}, use_global_device_ids=true, to_apply=%region_13.14 | all-reduce | flops 4096 | bytes 32768 | tf_op jit(solution)/shard_map/psum | solution.py:65
  475.5 12.4 %fusion.2 = bf16[8192,1024]{0,1:T(8,128)(2,1)} fusion(bf16[2,96,8192]{2,1,0:T(8,128)(2,1)} %all-gather.4.cloned.1.call-done, f32[2,96,1024]{2,1,0:T(8,128)S(1)} %get-tuple-element.20, f32[1,96,1024]{2,1,0:T(8,128)S(1)} %fusion.4, f32[1,96,1024]{2,1,0:T(8,128)} %copy-done.1, f32[2,1024]{1,0:T(2,128)S(1)} %get-tuple-element.21, ...), kind=kOutput, calls=%fused_computation.3 | convolution fusion | flops 3231186944 | bytes 21528576 | tf_op jit(solution)/shard_map/dot_general | solution.py:74
  490.6 41.4 %all-reduce = (f32[]{:T(128)}, f32[]{:T(128)}) all-reduce(f32[]{:T(128)S(6)} %add.47, f32[]{:T(128)S(6)} %sub.40), channel_id=1, replica_groups=mesh['dp'=4,'feat'=8] {'dp','feat'}, use_global_device_ids=true, to_apply=%region_9.10 | all-reduce | flops 2 | bytes 16 | tf_op jit(solution)/shard_map/psum | solution.py:51
  533.3 0.7 bitcast_select_fusion
  534.0 232.7 %reduce-scatter.2.cloned.1.call-done = bf16[2048,1024]{0,1:T(8,128)(2,1)} async-done(((bf16[8192,1024]{0,1:T(8,128)(2,1)}), bf16[2048,1024]{0,1:T(8,128)(2,1)}) %reduce-scatter.2.cloned.1.call-update) | async-done | bytes 4194320 | tf_op jit(solution)/shard_map/reduce_scatter | solution.py:73
  766.7 6.6 convert_multiply_fusion
  773.4 9.2 %copy.6 = f32[2048,1024]{1,0:T(8,128)} copy(f32[2048,1024]{0,1:T(8,128)} %convert_multiply_fusion) | data formatting | bytes 16777216
  (21 shorter events, 1.3 us)
Async XLA Ops:
  7.2 37.8 %all-gather.4.cloned.1.call-start = ((), (), s32[]{:S(2)}) async-start(), calls=%async_computation.1 | async-start | bytes 3538944 | tf_op jit(solution)/shard_map/all_gather | solution.py:18
  7.9 325.4 %all-gather.6.cloned.1.call-start = ((), (), s32[]{:S(2)}) async-start(), calls=%async_computation.2 | async-start | bytes 20971520 | tf_op jit(solution)/shard_map/all_gather | solution.py:22
  8.6 388.7 %all-gather.8.cloned.1.call-start = ((), (), s32[]{:S(2)}) async-start(), calls=%async_computation.3 | async-start | bytes 1966080 | tf_op jit(solution)/shard_map/all_gather | solution.py:32
  362.0 90.4 %all-reduce.4.cloned.1.call-start = ((), (), s32[]{:S(2)}) async-start(), calls=%async_computation.4 | async-start | bytes 589824 | tf_op jit(solution)/shard_map/psum | solution.py:34
  397.3 57.5 %copy-start = (bf16[2,384,1024]{2,1,0:T(8,128)(2,1)S(1)}, bf16[2,384,1024]{2,1,0:T(8,128)(2,1)}, u32[]{:S(2)}) copy-start(bf16[2,384,1024]{2,1,0:T(8,128)(2,1)} %all-gather.8.cloned.1.call-done) | copy-start | bytes 4718596
  400.3 366.4 %reduce-scatter.2.cloned.1.call-start = ((), (), s32[]{:S(2)}) async-start(), calls=%async_computation.5 | async-start | bytes 20971520 | tf_op jit(solution)/shard_map/reduce_scatter | solution.py:73
  455.8 0.7 copy-start.1
  487.9 1.4 copy-start.2
Sparse Core Ops, SparseCore 0:
  9.9 35.0 all-gather.3
  46.5 286.7 all-gather.5
  362.1 35.1 all-gather.7
  400.5 51.9 all-reduce.3
  488.0 278.6 reduce-scatter.1
where the time goes:
time: 792 us; the launch traced here: 791 us
  waiting for transfers between devices  636 us (80%)
  blocking collectives  87.9 us (11%)
  matrix products  26.2 us (3%)
  between operations  19.5 us (2%)
  other arithmetic  11.4 us (1%)
  local copies, waits for them, and re-layouts  9.99 us (1%)
    all_gather x1, waiting for transfers between devices, per_device(): lax.all_gather(proj_weight, 'dp', axis=0, tiled=True)  288 us
    reduce_scatter x1, waiting for transfers between devices, per_device(): lax.psum_scatter(jnp.dot(stacked.T, flat_grad, preferred_element_type=jnp...  233 us
    psum x1, waiting for transfers between devices, per_device(): grams = lax.psum(gram_part, 'feat')  50.8 us
    psum x1, blocking collectives, per_device(): total_loss, off_sum = lax.psum((loss_term, off_term), ('dp', 'feat'))  41.4 us
    all_gather x1, waiting for transfers between devices, per_device(): gathered = lax.all_gather(clip_feats, 'feat', axis=2, tiled=True)  36.3 us
    all_gather x1, waiting for transfers between devices, per_device(): batch_all = lax.all_gather(quantized, 'dp', axis=1, tiled=True)  26.6 us
    psum x1, blocking collectives, per_device(): lax.psum((jnp.sum(grad_norm, axis=1), jnp.sum(grad_norm * normed, axis=1)...  18.7 us
  transfers between devices with their start and end apart: 5, of which 5 were waited for; matrix products, arithmetic and copies ran while one was open for 0% of the time, Pallas kernels for 0%

commit v1 on v0

--- a/solution.py
+++ b/solution.py
@@ -10,6 +10,18 @@
 grad_scale = 32.0
 
 
+def doubled_up(x, axis, dim):
+    ways, here, step = (lax.axis_size(axis), lax.axis_index(axis), x.shape[dim])
+    line, have = (x, 1)
+    while have < ways:
+        line = jnp.concatenate(
+            [line, lax.ppermute(line, axis, [(d, (d - have) % ways) for d in range(ways)])],
+            axis=dim,
+        )
+        have = 2 * have
+    return jnp.roll(line, here * step, axis=dim)
+
+
 def per_device(clip_feats, proj_weight):
     pairs = clip_feats.shape[1]
     width = clip_feats.shape[2]
@@ -18,9 +30,7 @@
     gathered = lax.all_gather(clip_feats, "feat", axis=2, tiled=True)
     stacked = gathered.reshape(2 * pairs, gathered.shape[2])
     projected = jnp.dot(
-        stacked,
-        lax.all_gather(proj_weight, "dp", axis=0, tiled=True),
-        preferred_element_type=jnp.float32,
+        stacked, doubled_up(proj_weight, "dp", 0), preferred_element_type=jnp.float32
     ).reshape(2, pairs, width)
     col_mean = lax.psum(jnp.sum(projected, axis=1), "dp")[:, None, :] / pair_count
     centered = projected - col_mean

time: 792 us -> 953 us (1.20)
  waiting for transfers between devices: 636 us -> 752 us
  local copies, waits for them, and re-layouts: 9.99 us -> 40.5 us
    ppermute x0 -> x2, waiting for transfers between devices: none -> 442 us  [doubled_up(): lax.ppermute(line, axis, [(d, (d - have) % ways) for d in range(ways)])]
    all_gather x1 -> x0, waiting for transfers between devices: 288 us -> none  [per_device(): lax.all_gather(proj_weight, 'dp', axis=0, tiled=True)]
    all_gather x1, waiting for transfers between devices: 36.3 us -> 0.01 us  [per_device(): gathered = lax.all_gather(clip_feats, 'feat', axis=2, tiled=True)]
    unnamed x7 -> x10, local copies, waits for them, and re-layouts: 9.99 us -> 32.9 us
  transfers between devices with their start and end apart: 5 -> 6, of which waited for: 5 -> 5; matrix products, arithmetic and copies ran while one was open for 0% -> 3% of each run, Pallas kernels for 0% -> 0%
where the time goes in v1:
time: 953 us; the launch traced here: 952 us
  waiting for transfers between devices  752 us (79%)
  blocking collectives  90.1 us (9%)
  local copies, waits for them, and re-layouts  40.5 us (4%)
  matrix products  24.2 us (3%)
  between operations  19.5 us (2%)
  other arithmetic  18.8 us (2%)
    ppermute x2, waiting for transfers between devices, doubled_up(): lax.ppermute(line, axis, [(d, (d - have) % ways) for d in range(ways)])  442 us
    reduce_scatter x1, waiting for transfers between devices, per_device(): lax.psum_scatter(jnp.dot(stacked.T, flat_grad, preferred_element_type=jnp...  233 us
    psum x1, waiting for transfers between devices, per_device(): grams = lax.psum(gram_part, 'feat')  51.5 us
    psum x1, blocking collectives, per_device(): total_loss, off_sum = lax.psum((loss_term, off_term), ('dp', 'feat'))  41.4 us
    unnamed x10, local copies, waits for them, and re-layouts  32.9 us
    all_gather x1, waiting for transfers between devices, per_device(): batch_all = lax.all_gather(quantized, 'dp', axis=1, tiled=True)  26.3 us
  transfers between devices with their start and end apart: 6, of which 5 were waited for; matrix products, arithmetic and copies ran while one was open for 3% of the time, Pallas kernels for 0%

profile of v1, /device:TPU:0, one launch (start us, length us, event | category | flops | bytes accessed | tf_op | source)
XLA Modules:
  0.0 952.1 jit_solution(18072599116478136054)
XLA Ops:
  7.2 5.1 collective-permute-start
  12.3 90.1 %collective-permute-done = bf16[2048,1024]{1,0:T(8,128)(2,1)} collective-permute-done((bf16[2048,1024]{1,0:T(8,128)(2,1)}, bf16[2048,1024]{1,0:T(8,128)(2,1)}, u32[]{:S(2)}, u32[]{:S(2)}) %collective-permute-start) | collective-permute-done | bytes 4194336 | tf_op jit(solution)/shard_map/ppermute | solution.py:18
  102.5 7.8 pad_maximum_fusion
  110.3 1.5 collective-permute-start.1
  111.9 4.6 constant_dynamic-update-slice_fusion.5
  116.4 4.6 constant_dynamic-update-slice_fusion.4
  121.0 351.6 %collective-permute-done.1 = bf16[4096,1024]{1,0:T(8,128)(2,1)} collective-permute-done((bf16[4096,1024]{1,0:T(8,128)(2,1)}, bf16[4096,1024]{1,0:T(8,128)(2,1)}, u32[]{:S(2)}, u32[]{:S(2)}) %collective-permute-start.1) | collective-permute-done | bytes 8388640 | tf_op jit(solution)/shard_map/ppermute | solution.py:18
  472.6 7.6 constant_dynamic-update-slice_fusion.3
  480.2 2.4 constant_dynamic-update-slice_fusion.2
  482.5 4.6 constant_dynamic-update-slice_fusion.1
  487.1 7.6 constant_dynamic-update-slice_fusion
  494.7 8.5 fusion
  503.3 11.0 %psum.56 = f32[2,1024]{1,0:T(2,128)S(1)} all-reduce(f32[2,1024]{1,0:T(2,128)S(1)} %reduce_sum.72), channel_id=1, replica_groups=mesh['dp'=4,'feat'=8] {'dp'}, use_global_device_ids=true, to_apply=%region_1.2 | all-reduce | flops 2048 | bytes 16384 | tf_op jit(solution)/shard_map/psum | solution.py:35
  514.3 8.5 psum.57
  523.9 10.5 %psum.58 = f32[1024]{0:T(1024)S(1)} all-reduce(f32[1024]{0:T(1024)S(1)} %multiply_reduce_fusion.2), channel_id=1, replica_groups=mesh['dp'=4,'feat'=8] {'dp'}, use_global_device_ids=true, to_apply=%region_5.6 | all-reduce | flops 1024 | bytes 8192 | tf_op jit(solution)/shard_map/psum | solution.py:53
  534.4 26.3 %all-gather.5.cloned.1.call-done = bf16[2,384,1024]{2,1,0:T(8,128)(2,1)} async-done(((bf16[2,96,1024]{2,1,0:T(8,128)(2,1)}), bf16[2,384,1024]{2,1,0:T(8,128)(2,1)}) %all-gather.5.cloned.1.call-update) | async-done | bytes 1572880 | tf_op jit(solution)/shard_map/all_gather | solution.py:42
  560.7 2.8 fusion.17
  564.2 51.5 %all-reduce.4.cloned.1.call-done = f32[2,96,384]{2,1,0:T(8,128)} async-done(((f32[2,96,384]{2,1,0:T(8,128)}), f32[2,96,384]{2,1,0:T(8,128)}) %all-reduce.4.cloned.1.call-update) | async-done | bytes 294928 | tf_op jit(solution)/shard_map/psum | solution.py:44
  619.8 18.7 %all-reduce.1 = (f32[2,1024]{1,0:T(2,128)S(1)}, f32[2,1024]{1,0:T(2,128)S(1)}) all-reduce(f32[2,1024]{1,0:T(2,128)S(1)} %get-tuple-element.9, f32[2,1024]{1,0:T(2,128)S(1)} %get-tuple-element.8), channel_id=1, replica_groups=mesh['dp'=4,'feat'=8] {'dp'}, use_global_device_ids=true, to_apply=%region_13.14 | all-reduce | flops 4096 | bytes 32768 | tf_op jit(solution)/shard_map/psum | solution.py:75
  638.6 10.0 %fusion.2 = bf16[8192,1024]{0,1:T(8,128)(2,1)} fusion(bf16[2,96,8192]{2,1,0:T(8,128)(2,1)} %all-gather.3.cloned.1.call-done, f32[2,96,1024]{2,1,0:T(8,128)S(1)} %bitcast.48, f32[1,96,1024]{2,1,0:T(8,128)S(1)} %fusion.4, f32[1,96,1024]{2,1,0:T(8,128)S(1)} %fusion.6, f32[2,1024]{1,0:T(2,128)S(1)} %get-tuple-element.19, f32[2,1024]{1,0:T(2,128)S(1)} %get-tuple-element.20, ...), kind=kOutput, calls=%fused_computation.3 | convolution fusion | flops 3231186944 | bytes 21528576 | tf_op jit(solution)/shard_map/dot_general | solution.py:84
  651.3 41.4 %all-reduce = (f32[]{:T(128)}, f32[]{:T(128)}) all-reduce(f32[]{:T(128)S(6)} %add.59, f32[]{:T(128)S(6)} %sub.45), channel_id=1, replica_groups=mesh['dp'=4,'feat'=8] {'dp','feat'}, use_global_device_ids=true, to_apply=%region_9.10 | all-reduce | flops 2 | bytes 16 | tf_op jit(solution)/shard_map/psum | solution.py:61
  694.8 232.7 %reduce-scatter.2.cloned.1.call-done = bf16[2048,1024]{0,1:T(8,128)(2,1)} async-done(((bf16[8192,1024]{0,1:T(8,128)(2,1)}), bf16[2048,1024]{0,1:T(8,128)(2,1)}) %reduce-scatter.2.cloned.1.call-update) | async-done | bytes 4194320 | tf_op jit(solution)/shard_map/reduce_scatter | solution.py:83
  927.5 6.6 convert_multiply_fusion
  934.1 9.2 copy.6
  (28 shorter events, 7.4 us)
Async XLA Ops:
  7.2 487.5 %all-gather.3.cloned.1.call-start = ((), (), s32[]{:S(2)}) async-start(), calls=%async_computation.1 | async-start | bytes 3538944 | tf_op jit(solution)/shard_map/all_gather | solution.py:30
  7.2 95.2 %collective-permute-start = (bf16[2048,1024]{1,0:T(8,128)(2,1)}, bf16[2048,1024]{1,0:T(8,128)(2,1)}, u32[]{:S(2)}, u32[]{:S(2)}) collective-permute-start(bf16[2048,1024]{1,0:T(8,128)(2,1)} %param.3), channel_id=1, source_target_pairs={{0,24},{8,0},{16,8},{24,16},{1,25},{9,1},{17,9},{25,17},{2,26},{10... | collective-permute-start | bytes 12582920 | tf_op jit(solution)/shard_map/ppermute | solution.py:18
  110.3 362.3 %collective-permute-start.1 = (bf16[4096,1024]{1,0:T(8,128)(2,1)}, bf16[4096,1024]{1,0:T(8,128)(2,1)}, u32[]{:S(2)}, u32[]{:S(2)}) collective-permute-start(bf16[4096,1024]{1,0:T(8,128)(2,1)} %pad_maximum_fusion), channel_id=1, source_target_pairs={{0,16},{8,24},{16,0},{24,8},{1,17},{9,25},{17,1},{25,9},{2,18},{10... | collective-permute-start | bytes 25165832 | tf_op jit(solution)/shard_map/ppermute | solution.py:18
  111.8 448.9 %all-gather.5.cloned.1.call-start = ((), (), s32[]{:S(2)}) async-start(), calls=%async_computation.2 | async-start | bytes 1966080 | tf_op jit(solution)/shard_map/all_gather | solution.py:42
  121.0 359.2 %copy-start = (bf16[2048,1024]{1,0:T(8,128)(2,1)S(1)}, bf16[2048,1024]{1,0:T(8,128)(2,1)}, u32[]{:S(2)}) copy-start(bf16[2048,1024]{1,0:T(8,128)(2,1)} %param.3) | copy-start | bytes 12582916
  523.8 92.0 %all-reduce.4.cloned.1.call-start = ((), (), s32[]{:S(2)}) async-start(), calls=%async_computation.3 | async-start | bytes 589824 | tf_op jit(solution)/shard_map/psum | solution.py:44
  563.6 363.9 %reduce-scatter.2.cloned.1.call-start = ((), (), s32[]{:S(2)}) async-start(), calls=%async_computation.4 | async-start | bytes 20971520 | tf_op jit(solution)/shard_map/reduce_scatter | solution.py:83
  648.6 1.4 copy-start.1
Sparse Core Ops, SparseCore 0:
  111.9 33.3 all-gather.2
  523.9 36.7 all-gather.4
  563.8 51.9 all-reduce.3
  648.8 278.6 reduce-scatter.1
